TPU v7x, 32 devices: a whole 2x2x4 slice. The times are simulated.
32 devices in a mesh: blk: 8 (over y, x, core), team: 4 (over z).
Axes of the slice: x: 2, y: 2, z: 4, core: 2. Of those that a mesh axis runs over, the one named last changes fastest.
Arguments:
- features: bfloat16 [8192, 128], P(('blk', 'team')), may hold values from -0.796875 to 0.796875
- left_vectors: bfloat16 [8192, 128], P(('blk', 'team')), may hold values from -0.8984375 to 0.8984375
- right_vectors: bfloat16 [8192, 128], P(('blk', 'team')), may hold values from -0.8984375 to 0.8984375
Outputs:
- feature_grad: float32 [8192, 128], P(('blk', 'team'))
All inputs are finite; a program needn't handle non-finite values.
Results may differ from a plain program's by a relative error of at most 0.0039.
Values may be sent and summed in bfloat16 or wider, within the bound.
A program may use at most 64 MiB of HBM per device.

v0:
```python
import functools
import math

import jax
import jax.numpy as jnp
from jax import lax
from jax.experimental import pallas as pl
from jax.experimental.pallas import tpu as pltpu
from jax.sharding import PartitionSpec as P

MESH = pl.DeviceIdType.MESH
LOG2E = math.log2(math.e)
RATE = math.sqrt(5.0) * LOG2E
GAIN = -(5.0 / 3.0) / LOG2E
NT = (((1,), (1,)), ((), ()))


def flip(index, bits):
    step = 1
    while step <= bits:
        if bits & step:
            index = index + step - 2 * step * ((index // step) % 2)
        step *= 2
    return index


def columns(norm, lane, first, ones):
    high = norm.astype(jnp.bfloat16).astype(jnp.float32)
    rest = norm - high
    mid = rest.astype(jnp.bfloat16).astype(jnp.float32)
    low = rest - mid
    out = jnp.where((lane >= ones) & (lane < ones + 3), 1.0, 0.0)
    for place, term in enumerate((high, mid, low)):
        out = jnp.where(lane == first + place, term, out)
    return out.astype(jnp.bfloat16)


def kernel(
    planes, teams, tile, split, x_hbm, l_hbm, r_hbm, out_ref, grad_in,
    own, tgt, src, tgt_aug, src_aug, acc, grad_out, mine_out, out_sem,
    load_sem, tgt_send, tgt_recv, z_send, z_recv, p_send, p_recv, g_send, g_recv,
):
    blk, team = lax.axis_index("blk"), lax.axis_index("team")
    plane, core = blk // 2, blk % 2
    rows, feat = x_hbm.shape

    loads = [
        pltpu.make_async_copy(ref, own.at[i], load_sem.at[i])
        for i, ref in enumerate((x_hbm, l_hbm, r_hbm))
    ]
    for load in loads:
        load.start()

    partner = (plane * 2 + 1 - core, team)
    plane_peer = [(flip(plane, k) * 2 + core, team) for k in range(planes)]
    peers = [partner] + plane_peer[1:]
    barrier = pltpu.get_barrier_semaphore()
    for peer in peers:
        pl.semaphore_signal(barrier, inc=1, device_id=peer, device_id_type=MESH)
    for step in (1, -1):
        @pl.when((team + step >= 0) & (team + step < teams))
        def _():
            pl.semaphore_signal(barrier, inc=1, device_id=(blk, team + step), device_id_type=MESH)

    def remote(source, target, send, recv, peer):
        return pltpu.make_async_remote_copy(
            src_ref=source, dst_ref=target, send_sem=send, recv_sem=recv,
            device_id=peer, device_id_type=MESH,
        )

    to_plane = [None] + [
        remote(own, tgt.at[k - 1], tgt_send.at[k], tgt_recv.at[k], plane_peer[k])
        for k in range(1, planes)
    ]
    size = rows // split
    left, right = team, teams - 1 - team
    both = jnp.minimum(left, right)

    def position(n):
        paired = n <= 2 * both
        far = jnp.where(paired, (n + 1) // 2, n - both)
        sign = jnp.where(paired, 1 - 2 * (n % 2), jnp.where(left < right, 1, -1))
        return team + sign * far, -sign

    order = [None] + [position(n) for n in range(1, teams)]

    def part_of(ref, h):
        return ref.at[:, pl.ds(h * size, size)]

    def line_copy(source, shard, h, send, step):
        return remote(
            part_of(source, h), part_of(src.at[2 * shard], h), send, z_recv.at[shard, h],
            (blk, team + step),
        )

    def can_go(step):
        return (team + step >= 0) & (team + step < teams)

    def own_copy(step, h):
        return line_copy(own, team, h, z_send.at[team if step > 0 else teams, h], step)

    def forward(n, h):
        shard, step = order[n]
        return line_copy(src.at[2 * shard], shard, h, z_send.at[shard, h], step)

    def relay(n, h):
        shard = order[n][0]
        return remote(
            part_of(src.at[2 * shard], h), part_of(src.at[2 * shard + 1], h),
            p_send.at[shard, h], p_recv.at[shard, h], partner,
        )

    mine = 2 * team
    to_partner = remote(own, src.at[mine + 1], p_send.at[team, 0], p_recv.at[team, 0], partner)
    to_owner = [None] + [
        remote(grad_out.at[k - 1], grad_in.at[k - 1], g_send.at[k], g_recv.at[k], plane_peer[k])
        for k in range(1, planes)
    ]

    for load in loads:
        load.wait()
    on_line = jnp.minimum(team, 1) + jnp.minimum(teams - 1 - team, 1)
    pl.semaphore_wait(barrier, len(peers) + on_line)
    to_partner.start()
    for h in range(split):
        for step in (1, -1):
            @pl.when(can_go(step))
            def _():
                own_copy(step, h).start()
    for k in range(1, planes):
        to_plane[k].start()

    def norm_of(x):
        xf = x.astype(jnp.float32)
        return jnp.sum(xf * xf, axis=1, keepdims=True)


    def raw_target(k):
        return own if k == 0 else tgt.at[k - 1]

    def raw_source(s):
        return own if s is mine else src.at[s]

    lane = lax.broadcasted_iota(jnp.int32, (rows, feat), 1)

    def prepare_target(k):
        x = raw_target(k)[0]
        tgt_aug[k, :, :feat] = x * jnp.bfloat16(-2.0)
        tgt_aug[k, :, feat:] = columns(norm_of(x), lane, 0, 3)

    def prepare_source(s):
        x = raw_source(s)[0]
        src_aug[s, :, :feat] = x
        src_aug[s, :, feat:] = columns(norm_of(x), lane, 3, 0)

    def tile_pair(k, s, i, j, first):
        ti, sj = pl.ds(i, tile), pl.ds(j, tile)
        target, source = raw_target(k), raw_source(s)
        src_a = src_aug[s, sj, :]
        dist = lax.dot_general(tgt_aug[k, ti, :], src_a, NT, preferred_element_type=jnp.float32)
        couple = lax.dot_general(
            jnp.concatenate([target[1, ti, :], target[2, ti, :]], axis=1),
            jnp.concatenate([source[2, sj, :], source[1, sj, :]], axis=1),
            NT, preferred_element_type=jnp.float32,
        )
        dist = jnp.maximum(dist, 1e-30)
        power = dist * lax.rsqrt(dist) * (-RATE)
        weight = ((LOG2E - power) * jnp.exp2(power) * couple).astype(jnp.bfloat16)
        part = jnp.dot(weight, src_a, preferred_element_type=jnp.float32)
        if first:
            acc[k, ti, :] = part
        else:
            acc[k, ti, :] += part

    def pair(k, s):
        if rows == tile:
            tile_pair(k, s, 0, 0, s is mine)
            return

        @pl.loop(0, rows // tile)
        def _(i):
            i = pl.multiple_of(i * tile, tile)
            tile_pair(k, s, i, 0, s is mine)

            @pl.loop(1, rows // tile)
            def _(j):
                tile_pair(k, s, i, pl.multiple_of(j * tile, tile), False)

    def gradient(k):
        total = acc[k]
        x = raw_target(k)[0].astype(jnp.float32)
        return GAIN * (total[:, feat:feat + 1] * x - total[:, :feat])

    inner = both > 0

    def receive(n, h):
        line_copy(own, order[n][0], h, z_send.at[0, 0], 0).wait_recv()

        @pl.when(can_go(order[n][1]))
        def _():
            forward(n, h).start()
        relay(n, h).start()

    def receive_when(condition, n, halves=range(split)):
        if n < teams:
            @pl.when(condition)
            def _():
                for h in halves:
                    receive(n, h)

    def take(n):
        prepare_source(2 * order[n][0])
        return 2 * order[n][0]

    def take_partner(n):
        for h in range(split):
            relay(n, h).wait_recv()
        prepare_source(2 * order[n][0] + 1)
        return 2 * order[n][0] + 1

    prepare_target(0)
    prepare_source(mine)
    pair(0, mine)
    to_partner.wait_recv()
    next_door = mine + 1
    prepare_source(next_door)
    pair(0, next_door)
    if teams > 1:
        for h in range(split):
            receive(1, h)
        receive_when(inner, 2)
        first = take(1)
        pair(0, first)
    for k in range(1, planes):
        to_plane[k].wait_recv()
        if k == planes - 1:
            receive_when(inner, 3)
        prepare_target(k)
        pair(k, mine)
        pair(k, next_door)
        if teams > 1:
            pair(k, first)
    outer = jnp.logical_not(inner)
    receive_when(outer, 2)
    for n in range(1, teams - 1):
        slot = take_partner(n)
        for k in range(planes):
            pair(k, slot)
        if n + 1 > 3:
            for h in range(split):
                receive(n + 1, h)
        elif n + 1 == 3:
            receive_when(outer, 3)
        slot = take(n + 1)
        for k in range(planes):
            pair(k, slot)
    if teams > 1:
        slot = take_partner(teams - 1)
    for k in reversed(range(planes)):
        if teams > 1:
            pair(k, slot)
        if k:
            grad_out[k - 1] = gradient(k).astype(jnp.bfloat16)
            to_owner[k].start()
    mine_out[...] = gradient(0)
    put = pltpu.make_async_copy(mine_out, out_ref, out_sem)
    put.start()
    for k in reversed(range(1, planes)):
        to_owner[k].wait_recv()
    put.wait()
    for copy in to_plane[1:] + [to_partner] + to_owner[1:]:
        copy.wait_send()
    for h in range(split):
        for step in (1, -1):
            @pl.when(can_go(step))
            def _():
                own_copy(step, h).wait_send()
        for n in range(1, teams):
            relay(n, h).wait_send()

            @pl.when(can_go(order[n][1]))
            def _():
                forward(n, h).wait_send()


def local(planes, teams, features, left_vectors, right_vectors):
    rows, feat = features.shape
    kind = jnp.bfloat16
    dma = pltpu.SemaphoreType.DMA
    tile, split = min(rows, 256), 2
    partial, received = pl.pallas_call(
        functools.partial(kernel, planes, teams, tile, split),
        out_shape=(
            jax.ShapeDtypeStruct((rows, feat), jnp.float32),
            jax.ShapeDtypeStruct((max(planes - 1, 1), rows, feat), kind),
        ),
        in_specs=[pl.BlockSpec(memory_space=pl.ANY)] * 3,
        out_specs=(pl.BlockSpec(memory_space=pl.ANY),) * 2,
        scratch_shapes=[
            pltpu.VMEM((3, rows, feat), kind),
            pltpu.VMEM((max(planes - 1, 1), 3, rows, feat), kind),
            pltpu.VMEM((2 * teams, 3, rows, feat), kind),
            pltpu.VMEM((planes, rows, 2 * feat), kind),
            pltpu.VMEM((2 * teams, rows, 2 * feat), kind),
            pltpu.VMEM((planes, rows, 2 * feat), jnp.float32),
            pltpu.VMEM((max(planes - 1, 1), rows, feat), kind),
            pltpu.VMEM((rows, feat), jnp.float32),
            dma,
            dma((3,)),
            dma((planes,)), dma((planes,)),
            dma((teams + 1, split)), dma((teams, split)),
            dma((teams, split)), dma((teams, split)),
            dma((planes,)), dma((planes,)),
        ],
        compiler_params=pltpu.CompilerParams(collective_id=0, has_side_effects=True),
    )(features, left_vectors, right_vectors)
    for k in range(planes - 1):
        partial = partial + received[k].astype(jnp.float32)
    return partial


def solution(mesh):
    spec = P(("blk", "team"), None)
    planes, teams = mesh.shape["blk"] // 2, mesh.shape["team"]
    return jax.shard_map(
        functools.partial(local, planes, teams), mesh=mesh,
        in_specs=(spec, spec, spec), out_specs=spec, check_vma=False,
    )
```

profile of v0, /device:TPU:0, one launch (start us, length us, event | category | flops | bytes accessed | tf_op | source)
XLA Modules:
  0.0 28.8 jit_solution(13140066107309516952)
XLA Ops:
  0.0 27.1 %shard_map.37 = (f32[256,128]{1,0:T(8,128)}, bf16[3,256,128]{2,1,0:T(8,128)(2,1)}) custom-call(bf16[256,128]{1,0:T(8,128)(2,1)} %x_hbm.1, bf16[256,128]{1,0:T(8,128)(2,1)} %l_hbm.1, bf16[256,128]{1,0:T(8,128)(2,1)} %r_hbm.1), custom_call_target="tpu_custom_call" | custom-call | tf_op jit(solution)/shard_map/pallas_call | solution.py:291
  27.1 1.7 %convert_add_fusion = f32[256,128]{1,0:T(8,128)} fusion(f32[256,128]{1,0:T(8,128)} %get-tuple-element.7, bf16[3,256,128]{2,1,0:T(8,128)(2,1)} %get-tuple-element.8), kind=kLoop, calls=%fused_computation | loop fusion | flops 196608 | bytes 458752 | tf_op jit(solution)/shard_map/add | solution.py:318
where the time goes:
time: 28.9 us; the launch traced here: 28.8 us
  Pallas kernels  27.1 us (94%)
  other arithmetic  1.65 us (6%)
    pallas_call x1, Pallas kernels, local(): pl.pallas_call(functools.partial(kernel, planes, teams, tile, split), out...  27.1 us
    add x1, other arithmetic, local(): partial = partial + received[k].astype(jnp.float32)  1.65 us

commit v1 on v0

v1 whole, which is shorter than its diff:
```python
import functools
import math

import jax
import jax.numpy as jnp
from jax import lax
from jax.experimental import pallas as pl
from jax.experimental.pallas import tpu as pltpu
from jax.sharding import PartitionSpec as P

MESH = pl.DeviceIdType.MESH
LOG2E = math.log2(math.e)
RATE = math.sqrt(5.0) * LOG2E
GAIN = -(5.0 / 3.0) / LOG2E
NT = (((1,), (1,)), ((), ()))
ONES = 16


def flip(index, bits):
    step = 1
    while step <= bits:
        if bits & step:
            index = index + step - 2 * step * ((index // step) % 2)
        step *= 2
    return index


def columns(norm, lane, first, ones):
    high = norm.astype(jnp.bfloat16).astype(jnp.float32)
    rest = norm - high
    mid = rest.astype(jnp.bfloat16).astype(jnp.float32)
    low = rest - mid
    out = jnp.where((lane >= ones) & (lane < ones + 3), 1.0, 0.0)
    for place, term in enumerate((high, mid, low)):
        out = jnp.where(lane == first + place, term, out)
    return out.astype(jnp.bfloat16)


def goes_up(teams, i):
    return 2 * i <= teams - 2


def goes_down(teams, i):
    return 2 * i > teams


def above(teams, i, t):
    return (t > i) & (t <= teams - 1 - i)


def below(teams, i, t):
    return (t < i) & (t > teams - 1 - i)


def kernel(
    planes, teams, parts, x_hbm, l_hbm, r_hbm, out_ref,
    own, tgt, src, tgt_left, tgt_turned, src_right, acc, turned,
    core_out, core_in, plane_out, plane_in, line_out, line_in, mine_out,
    out_sem, load_sem, core_send, core_recv, plane_send, plane_recv,
    own_send, line_send, line_recv, csum_send, csum_recv,
    psum_send, psum_recv, lsum_send, lsum_recv,
):
    blk, team = lax.axis_index("blk"), lax.axis_index("team")
    plane, core = blk // 2, blk % 2
    rows, feat = x_hbm.shape
    half, size = rows // 2, rows // parts
    bf16, f32 = jnp.bfloat16, jnp.float32

    loads = [
        pltpu.make_async_copy(ref, own.at[i], load_sem.at[i])
        for i, ref in enumerate((x_hbm, l_hbm, r_hbm))
    ]
    for load in loads:
        load.start()

    partner = (plane * 2 + 1 - core, team)
    peer = [(flip(plane, k) * 2 + core, team) for k in range(planes)]
    single = [k for k in range(1, planes) if k & (k - 1) == 0]
    joint = [k for k in range(1, planes) if k & (k - 1)]
    barrier = pltpu.get_barrier_semaphore()
    near = [partner] + [peer[k] for k in single]
    for device in near:
        pl.semaphore_signal(barrier, inc=1, device_id=device, device_id_type=MESH)
    for step in (1, -1):
        @pl.when((team + step >= 0) & (team + step < teams))
        def _():
            pl.semaphore_signal(barrier, inc=1, device_id=(blk, team + step), device_id_type=MESH)

    def remote(source, target, send, recv, device):
        return pltpu.make_async_remote_copy(
            src_ref=source, dst_ref=target, send_sem=send, recv_sem=recv,
            device_id=device, device_id_type=MESH,
        )

    def raw(k, c):
        return own if (k, c) == (0, 0) else tgt.at[k, c]

    def part(ref, h, length):
        return ref.at[:, pl.ds(h * length, length)]

    def plane_copy(k, h):
        if k in single:
            source, device = own, peer[k]
        else:
            low = k & -k
            rest = k ^ low
            if h and rest in single:
                source, device = raw(low, 0), peer[rest]
            else:
                source, device = raw(rest, 0), peer[low]
        return remote(
            part(source, h, half), part(tgt.at[k, 0], h, half),
            plane_send.at[k, h], plane_recv.at[k, h], device,
        )

    def core_copy(k):
        return remote(raw(k, 0), tgt.at[k, 1], core_send.at[k], core_recv.at[k], partner)

    sources = [i for i in range(teams) if goes_up(teams, i) or goes_down(teams, i)]
    sources.sort(key=lambda i: (min(i, teams - 1 - i), i))

    def direction(i):
        return 1 if goes_up(teams, i) else -1

    def uses(i, t):
        return above(teams, i, t) if goes_up(teams, i) else below(teams, i, t)

    def passes(i):
        return uses(i, team) & uses(i, team + direction(i))

    def line_copy(i, q):
        return remote(
            part(src.at[i], q, size), part(src.at[i], q, size),
            line_send.at[i, q], line_recv.at[i, q], (blk, team + direction(i)),
        )

    def own_copy(step, q):
        return remote(
            part(own, q, size), part(src.at[team], q, size),
            own_send.at[q], line_recv.at[team, q], (blk, team + step),
        )

    rises = goes_up(teams, team)
    sinks = goes_down(teams, team)

    def send_own(qs):
        for step, condition in ((1, rises), (-1, sinks)):
            @pl.when(condition)
            def _():
                for q in qs:
                    own_copy(step, q).start()

    def pass_on(q):
        for i in sources:
            @pl.when(passes(i))
            def _():
                line_copy(i, q).wait_recv()
                line_copy(i, q).start()

    for load in loads:
        load.wait()
    on_line = jnp.minimum(team, 1) + jnp.minimum(teams - 1 - team, 1)
    pl.semaphore_wait(barrier, len(near) + on_line)
    edge = (team == 0) | (team == teams - 1)
    send_own(range(1))

    @pl.when(edge)
    def _():
        send_own(range(1, parts))
    for n, k in enumerate(single):
        plane_copy(k, 1 - n % 2).start()
    core_copy(0).start()
    for n, k in enumerate(single):
        plane_copy(k, n % 2).start()

    lane = lax.broadcasted_iota(jnp.int32, (rows, feat), 1)
    one_row = jnp.where(lax.broadcasted_iota(jnp.int32, (ONES, rows), 0) == 0, 1.0, 0.0).astype(bf16)

    def norm_of(x):
        xf = x.astype(f32)
        return jnp.sum(xf * xf, axis=1, keepdims=True)

    def prepare_target(k, c):
        x = raw(k, c)[0]
        tgt_left[k, c, :, :feat] = x * bf16(-2.0)
        tgt_left[k, c, :, feat:] = columns(norm_of(x), lane, 0, 3)
        tgt_turned[k, c, :feat] = x.astype(f32).T.astype(bf16)
        tgt_turned[k, c, feat:] = one_row

    def prepare_source(ref, slot):
        x = ref[0]
        src_right[slot, :, :feat] = x
        src_right[slot, :, feat:] = columns(norm_of(x), lane, 3, 0)

    mine = teams

    def pair(k, c, ref, slot, add, first):
        right = src_right[slot]
        target = raw(k, c)
        dist = lax.dot_general(tgt_left[k, c], right, NT, preferred_element_type=f32)
        couple = lax.dot_general(
            jnp.concatenate([target[1], target[2]], axis=1),
            jnp.concatenate([ref[2], ref[1]], axis=1),
            NT, preferred_element_type=f32,
        )
        dist = jnp.maximum(dist, 1e-30)
        power = dist * lax.rsqrt(dist) * (-RATE)
        weight = ((LOG2E - power) * jnp.exp2(power) * couple).astype(bf16)
        back = jnp.dot(tgt_turned[k, c], weight, preferred_element_type=f32)
        if first:
            turned[slot] = back
        else:
            turned[slot] += back
        if add is not None:
            forth = jnp.dot(weight, right, preferred_element_type=f32)
            if add:
                acc[k, c] += forth
            else:
                acc[k, c] = forth

    def gradient(k, c):
        total = acc[k, c]
        return GAIN * (total[:, feat:feat + 1] * raw(k, c)[0].astype(f32) - total[:, :feat])

    def turned_gradient(ref, slot):
        total = turned[slot]
        fill = jnp.zeros((feat - ONES, rows), f32)
        whole = jnp.concatenate([total, fill], axis=0).T
        return GAIN * (whole[:, feat:feat + 1] * ref[0].astype(f32) - whole[:, :feat])

    def with_own(k, c):
        prepare_target(k, c)
        pair(k, c, own, mine, None, (k, c) == (0, 0))

    prepare_source(own, mine)
    with_own(0, 0)
    pass_on(0)
    core_copy(0).wait_recv()
    with_own(0, 1)

    started = set()
    arrived = set()

    def arrive(k, h):
        if (k, h) not in arrived:
            arrived.add((k, h))
            plane_copy(k, h).wait_recv()

    def hand_on(k):
        low = k & -k
        rest = k ^ low
        arrive(rest, 0)
        plane_copy(k, 0).start()
        arrive(low if rest in single else rest, 1)
        plane_copy(k, 1).start()

    middle = [q for q in range(1, parts)]
    for k in joint:
        if bin(k).count("1") == 2:
            hand_on(k)
    for q in middle[:-1]:
        pass_on(q)
    for k in single:
        arrive(k, 0)
        arrive(k, 1)
        core_copy(k).start()
    for k in single:
        with_own(k, 0)
    for q in middle[-1:]:
        pass_on(q)

    @pl.when(jnp.logical_not(edge))
    def _():
        send_own(range(1, parts))
    for k in single:
        core_copy(k).wait_recv()
        with_own(k, 1)
    for k in joint:
        if bin(k).count("1") > 2:
            hand_on(k)
        arrive(k, 0)
        arrive(k, 1)
        core_copy(k).start()
        with_own(k, 0)
    for k in joint:
        core_copy(k).wait_recv()
        with_own(k, 1)

    def to_owner(i):
        return remote(
            line_out.at[i], line_in.at[team], lsum_send.at[i], lsum_recv.at[team], (blk, i),
        )

    for n, i in enumerate(sources):
        @pl.when(uses(i, team))
        def _():
            @pl.when(jnp.logical_not(passes(i)))
            def _():
                for q in range(parts):
                    line_copy(i, q).wait_recv()
            prepare_source(src.at[i], i)
            for k in reversed(range(planes)):
                for c in (1, 0):
                    pair(k, c, src.at[i], i, n > 0, (k, c) == (planes - 1, 1))
            line_out[i] = turned_gradient(src.at[i], i).astype(bf16)
            to_owner(i).start()

    def csum_copy(k):
        return remote(core_out.at[k], core_in.at[k], csum_send.at[k], csum_recv.at[k], partner)

    def psum_copy(k):
        return remote(plane_out.at[k - 1], plane_in.at[k - 1], psum_send.at[k], psum_recv.at[k], peer[k])

    mine_out[...] = turned_gradient(own, mine)

    @pl.when(team > 0)
    def _():
        for k in reversed(range(planes)):
            core_out[k] = gradient(k, 1).astype(bf16)
            csum_copy(k).start()
        for k in reversed(range(1, planes)):
            csum_copy(k).wait_recv()
            plane_out[k - 1] = (gradient(k, 0) + core_in[k].astype(f32)).astype(bf16)
            psum_copy(k).start()
        csum_copy(0).wait_recv()
        mine_out[...] += gradient(0, 0) + core_in[0].astype(f32)
        for k in range(1, planes):
            psum_copy(k).wait_recv()
            mine_out[...] += plane_in[k - 1].astype(f32)

    def gives(j):
        return (rises & above(teams, team, j)) | (sinks & below(teams, team, j))

    for j in range(teams):
        @pl.when(gives(j))
        def _():
            remote(line_out.at[j], line_in.at[j], lsum_send.at[j], lsum_recv.at[j], partner).wait_recv()
            mine_out[...] += line_in[j].astype(f32)
    put = pltpu.make_async_copy(mine_out, out_ref, out_sem)
    put.start()
    put.wait()

    for k in range(1, planes):
        for h in range(2):
            plane_copy(k, h).wait_send()
    for k in range(planes):
        core_copy(k).wait_send()
    for step, condition in ((1, rises), (-1, sinks)):
        @pl.when(condition)
        def _():
            for q in range(parts):
                own_copy(step, q).wait_send()
    for i in sources:
        @pl.when(passes(i))
        def _():
            for q in range(parts):
                line_copy(i, q).wait_send()

        @pl.when(uses(i, team))
        def _():
            to_owner(i).wait_send()

    @pl.when(team > 0)
    def _():
        for k in range(planes):
            csum_copy(k).wait_send()
            if k:
                psum_copy(k).wait_send()


def local(planes, teams, features, left_vectors, right_vectors):
    rows, feat = features.shape
    kind = jnp.bfloat16
    dma = pltpu.SemaphoreType.DMA
    parts = 4
    others = max(planes - 1, 1)
    return pl.pallas_call(
        functools.partial(kernel, planes, teams, parts),
        out_shape=jax.ShapeDtypeStruct((rows, feat), jnp.float32),
        in_specs=[pl.BlockSpec(memory_space=pl.ANY)] * 3,
        out_specs=pl.BlockSpec(memory_space=pl.ANY),
        scratch_shapes=[
            pltpu.VMEM((3, rows, feat), kind),
            pltpu.VMEM((planes, 2, 3, rows, feat), kind),
            pltpu.VMEM((teams, 3, rows, feat), kind),
            pltpu.VMEM((planes, 2, rows, 2 * feat), kind),
            pltpu.VMEM((planes, 2, feat + ONES, rows), kind),
            pltpu.VMEM((teams + 1, rows, 2 * feat), kind),
            pltpu.VMEM((planes, 2, rows, 2 * feat), jnp.float32),
            pltpu.VMEM((teams + 1, feat + ONES, rows), jnp.float32),
            pltpu.VMEM((planes, rows, feat), kind),
            pltpu.VMEM((planes, rows, feat), kind),
            pltpu.VMEM((others, rows, feat), kind),
            pltpu.VMEM((others, rows, feat), kind),
            pltpu.VMEM((teams, rows, feat), kind),
            pltpu.VMEM((teams, rows, feat), kind),
            pltpu.VMEM((rows, feat), jnp.float32),
            dma,
            dma((3,)),
            dma((planes,)), dma((planes,)),
            dma((planes, 2)), dma((planes, 2)),
            dma((parts,)),
            dma((teams, parts)), dma((teams, parts)),
            dma((planes,)), dma((planes,)),
            dma((planes,)), dma((planes,)),
            dma((teams,)), dma((teams,)),
        ],
        compiler_params=pltpu.CompilerParams(collective_id=0, has_side_effects=True),
    )(features, left_vectors, right_vectors)


def solution(mesh):
    spec = P(("blk", "team"), None)
    planes, teams = mesh.shape["blk"] // 2, mesh.shape["team"]
    return jax.shard_map(
        functools.partial(local, planes, teams), mesh=mesh,
        in_specs=(spec, spec, spec), out_specs=spec, check_vma=False,
    )
```

time: 28.9 us -> 32.8 us (1.13)
  the two profiles are of different devices: /device:TPU:0 before, /device:TPU:17 now
where the time goes in v1:
time: 32.8 us; the launch traced here: 32.6 us
  Pallas kernels  31.1 us (95%)
  local copies, waits for them, and re-layouts  1.57 us (5%)
    pallas_call x1, Pallas kernels, local(): pl.pallas_call(functools.partial(kernel, planes, teams, parts), out_shape...  31.1 us
    unnamed x1, local copies, waits for them, and re-layouts  1.57 us

profile of v1, /device:TPU:17, one launch (start us, length us, event | category | flops | bytes accessed | tf_op | source)
XLA Modules:
  0.0 32.6 jit_solution(1664241072803822489)
XLA Ops:
  0.0 31.1 %shard_map.37 = f32[256,128]{1,0:T(8,128)} custom-call(bf16[256,128]{1,0:T(8,128)(2,1)} %x_hbm.1, bf16[256,128]{1,0:T(8,128)(2,1)} %l_hbm.1, bf16[256,128]{1,0:T(8,128)(2,1)} %r_hbm.1), custom_call_target="tpu_custom_call" | custom-call | tf_op jit(solution)/shard_map/pallas_call | solution.py:377
  31.1 1.6 %copy.5 = f32[256,128]{1,0:T(8,128)} copy(f32[256,128]{1,0:T(8,128)} %shard_map.37) | data formatting | bytes 262144

commit v2 on v1

--- a/solution.py
+++ b/solution.py
@@ -36,27 +36,31 @@
     return out.astype(jnp.bfloat16)
 
 
-def goes_up(teams, i):
-    return 2 * i <= teams - 2
-
-
-def goes_down(teams, i):
-    return 2 * i > teams
-
-
-def above(teams, i, t):
-    return (t > i) & (t <= teams - 1 - i)
-
-
-def below(teams, i, t):
-    return (t < i) & (t > teams - 1 - i)
+def top(teams, i):
+    return teams - 1 - i - jnp.minimum(i, 1)
+
+
+def bottom(teams, i):
+    return jnp.maximum(teams - 1 - i, 1)
+
+
+def rises(teams, i):
+    return i + 1 <= top(teams, i)
+
+
+def sinks(teams, i):
+    return i - 1 >= bottom(teams, i)
+
+
+def uses(teams, i, t):
+    return ((t > i) & (t <= top(teams, i))) | ((t < i) & (t >= bottom(teams, i)))
 
 
 def kernel(
     planes, teams, parts, x_hbm, l_hbm, r_hbm, out_ref,
     own, tgt, src, tgt_left, tgt_turned, src_right, acc, turned,
-    core_out, core_in, plane_out, plane_in, line_out, line_in, mine_out,
-    out_sem, load_sem, core_send, core_recv, plane_send, plane_recv,
+    core_out, core_in, plane_out, plane_in, line_out, line_in,
+    load_sem, core_send, core_recv, plane_send, plane_recv,
     own_send, line_send, line_recv, csum_send, csum_recv,
     psum_send, psum_recv, lsum_send, lsum_recv,
 ):
@@ -97,6 +101,13 @@
 
     def part(ref, h, length):
         return ref.at[:, pl.ds(h * length, length)]
+
+    inputs = (x_hbm, l_hbm, r_hbm)
+
+    def straight(target, h, length, send, recv, device):
+        for i, ref in enumerate(inputs):
+            place = pl.ds(h * length, length)
+            remote(ref.at[place], target.at[i, place], send, recv, device).start()
 
     def plane_copy(k, h):
         if k in single:
@@ -116,17 +127,22 @@
     def core_copy(k):
         return remote(raw(k, 0), tgt.at[k, 1], core_send.at[k], core_recv.at[k], partner)
 
-    sources = [i for i in range(teams) if goes_up(teams, i) or goes_down(teams, i)]
-    sources.sort(key=lambda i: (min(i, teams - 1 - i), i))
-
     def direction(i):
-        return 1 if goes_up(teams, i) else -1
-
-    def uses(i, t):
-        return above(teams, i, t) if goes_up(teams, i) else below(teams, i, t)
+        return 1 if 2 * i < teams - 1 else -1
+
+    def goes(i):
+        near_end, far_end = min(i, teams - 1 - i), max(i, teams - 1 - i)
+        if i < far_end:
+            return far_end - near_end > 1 or i == 0
+        return far_end - near_end > 1 or 0 < near_end < far_end
+
+    sources = [i for i in range(teams) if teams > 1 and goes(i)]
+
+    def used(i):
+        return uses(teams, i, team)
 
     def passes(i):
-        return uses(i, team) & uses(i, team + direction(i))
+        return used(i) & uses(teams, i, team + direction(i))
 
     def line_copy(i, q):
         return remote(
@@ -140,38 +156,35 @@
             own_send.at[q], line_recv.at[team, q], (blk, team + step),
         )
 
-    rises = goes_up(teams, team)
-    sinks = goes_down(teams, team)
-
-    def send_own(qs):
-        for step, condition in ((1, rises), (-1, sinks)):
-            @pl.when(condition)
-            def _():
-                for q in qs:
-                    own_copy(step, q).start()
-
-    def pass_on(q):
+    ways = ((1, rises(teams, team)), (-1, sinks(teams, team)))
+
+    def pass_on(q, condition):
         for i in sources:
-            @pl.when(passes(i))
+            @pl.when(passes(i) & condition)
             def _():
                 line_copy(i, q).wait_recv()
                 line_copy(i, q).start()
 
+    on_line = jnp.minimum(team, 1) + jnp.minimum(teams - 1 - team, 1)
+    pl.semaphore_wait(barrier, len(near) + on_line)
+    for step, condition in ways:
+        @pl.when(condition)
+        def _():
+            for q in range(parts):
+                straight(
+                    src.at[team], q, size, own_send.at[q], line_recv.at[team, q], (blk, team + step),
+                )
+
+    def to_plane(k, h):
+        straight(tgt.at[k, 0], h, half, plane_send.at[k, h], plane_recv.at[k, h], peer[k])
+
+    for n, k in enumerate(single):
+        to_plane(k, 1 - n % 2)
+    straight(tgt.at[0, 1], 0, rows, core_send.at[0], core_recv.at[0], partner)
+    for n, k in enumerate(single):
+        to_plane(k, n % 2)
     for load in loads:
         load.wait()
-    on_line = jnp.minimum(team, 1) + jnp.minimum(teams - 1 - team, 1)
-    pl.semaphore_wait(barrier, len(near) + on_line)
-    edge = (team == 0) | (team == teams - 1)
-    send_own(range(1))
-
-    @pl.when(edge)
-    def _():
-        send_own(range(1, parts))
-    for n, k in enumerate(single):
-        plane_copy(k, 1 - n % 2).start()
-    core_copy(0).start()
-    for n, k in enumerate(single):
-        plane_copy(k, n % 2).start()
 
     lane = lax.broadcasted_iota(jnp.int32, (rows, feat), 1)
     one_row = jnp.where(lax.broadcasted_iota(jnp.int32, (ONES, rows), 0) == 0, 1.0, 0.0).astype(bf16)
@@ -228,17 +241,6 @@
         whole = jnp.concatenate([total, fill], axis=0).T
         return GAIN * (whole[:, feat:feat + 1] * ref[0].astype(f32) - whole[:, :feat])
 
-    def with_own(k, c):
-        prepare_target(k, c)
-        pair(k, c, own, mine, None, (k, c) == (0, 0))
-
-    prepare_source(own, mine)
-    with_own(0, 0)
-    pass_on(0)
-    core_copy(0).wait_recv()
-    with_own(0, 1)
-
-    started = set()
     arrived = set()
 
     def arrive(k, h):
@@ -254,56 +256,39 @@
         arrive(low if rest in single else rest, 1)
         plane_copy(k, 1).start()
 
-    middle = [q for q in range(1, parts)]
-    for k in joint:
-        if bin(k).count("1") == 2:
-            hand_on(k)
-    for q in middle[:-1]:
-        pass_on(q)
-    for k in single:
+    def relay(k):
         arrive(k, 0)
         arrive(k, 1)
         core_copy(k).start()
-    for k in single:
-        with_own(k, 0)
-    for q in middle[-1:]:
-        pass_on(q)
-
-    @pl.when(jnp.logical_not(edge))
-    def _():
-        send_own(range(1, parts))
-    for k in single:
-        core_copy(k).wait_recv()
-        with_own(k, 1)
-    for k in joint:
-        if bin(k).count("1") > 2:
-            hand_on(k)
-        arrive(k, 0)
-        arrive(k, 1)
-        core_copy(k).start()
-        with_own(k, 0)
-    for k in joint:
-        core_copy(k).wait_recv()
-        with_own(k, 1)
-
-    def to_owner(i):
-        return remote(
-            line_out.at[i], line_in.at[team], lsum_send.at[i], lsum_recv.at[team], (blk, i),
-        )
-
-    for n, i in enumerate(sources):
-        @pl.when(uses(i, team))
+
+    def take(i):
+        @pl.when(used(i))
         def _():
             @pl.when(jnp.logical_not(passes(i)))
             def _():
                 for q in range(parts):
                     line_copy(i, q).wait_recv()
             prepare_source(src.at[i], i)
-            for k in reversed(range(planes)):
-                for c in (1, 0):
-                    pair(k, c, src.at[i], i, n > 0, (k, c) == (planes - 1, 1))
-            line_out[i] = turned_gradient(src.at[i], i).astype(bf16)
-            to_owner(i).start()
+
+    def own_pairs(targets):
+        for k, c in targets:
+            prepare_target(k, c)
+            pair(k, c, own, mine, None, (k, c) == (0, 0))
+
+    def pairs(i, targets):
+        @pl.when(used(i))
+        def _():
+            for k, c in targets:
+                pair(k, c, src.at[i], i, i > 0, (k, c) == targets[0] and (k, c) in opening)
+
+    def to_owner(i):
+        return remote(
+            line_out.at[i], line_in.at[team], lsum_send.at[i], lsum_recv.at[team], (blk, i),
+        )
+
+    def give_back(i):
+        line_out[i] = turned_gradient(src.at[i], i).astype(bf16)
+        to_owner(i).start()
 
     def csum_copy(k):
         return remote(core_out.at[k], core_in.at[k], csum_send.at[k], csum_recv.at[k], partner)
@@ -311,41 +296,158 @@
     def psum_copy(k):
         return remote(plane_out.at[k - 1], plane_in.at[k - 1], psum_send.at[k], psum_recv.at[k], peer[k])
 
-    mine_out[...] = turned_gradient(own, mine)
-
-    @pl.when(team > 0)
-    def _():
-        for k in reversed(range(planes)):
+    always = team >= 0
+    low_half = team < teams // 2
+    close = [(0, 0), (0, 1)] + [(k, 0) for k in single]
+    across = [(k, 1) for k in single]
+    rest = [(k, c) for c in (0, 1) for k in joint]
+    opening = close[:1]
+    two = [k for k in joint if bin(k).count("1") == 2]
+    more = [k for k in joint if k not in two]
+
+    prepare_source(own, mine)
+    own_pairs(close[:1])
+    pass_on(0, always)
+    core_copy(0).wait_recv()
+    own_pairs(close[1:2])
+    for k in two:
+        hand_on(k)
+    for q in range(1, parts - 1):
+        pass_on(q, always)
+    pass_on(parts - 1, low_half)
+    for k in single:
+        relay(k)
+    pass_on(parts - 1, jnp.logical_not(low_half))
+    own_pairs(close[2:])
+
+    end = team == teams - 1
+
+    def relay_rest(condition):
+        @pl.when(condition)
+        def _():
+            for k in two:
+                for h in range(2):
+                    plane_copy(k, h).wait_recv()
+                core_copy(k).start()
+
+    relay_rest(end)
+    base = sources[:1]
+    inner = sources[1:-1]
+    final = sources[1:][-1:]
+    alone, joined = team == 0, team > 0
+
+    def own_and_base(targets):
+        @pl.when(alone)
+        def _():
+            own_pairs(targets)
+
+        @pl.when(joined)
+        def _():
+            own_pairs(targets)
+            for i in base:
+                for k, c in targets:
+                    pair(k, c, src.at[i], i, False, False)
+
+    for i in base:
+        take(i)
+        pairs(i, close)
+    relay_rest(jnp.logical_not(end))
+    for k in two:
+        arrived.update({(k, 0), (k, 1)})
+    for k in more:
+        hand_on(k)
+        relay(k)
+    for i in inner:
+        take(i)
+        pairs(i, close)
+    for k, c in across:
+        core_copy(k).wait_recv()
+    if across:
+        own_and_base(across)
+    for k, c in rest:
+        if c:
+            core_copy(k).wait_recv()
+
+    @pl.when(alone)
+    def _():
+        own_pairs(rest)
+
+    @pl.when(joined)
+    def _():
+        for k, c in rest:
+            prepare_target(k, c)
+            for i in base:
+                pair(k, c, src.at[i], i, False, False)
+        for i in base:
+            give_back(i)
+
+    @pl.when(joined)
+    def _():
+        for k, c in rest:
+            pair(k, c, own, mine, None, False)
+    for i in inner:
+        pairs(i, across + rest)
+
+        @pl.when(used(i))
+        def _():
+            give_back(i)
+
+    for i in final:
+        take(i)
+    order = list(reversed(range(planes)))
+    holds = used(final[0]) if final else team < 0
+
+    def hand_over():
+        for k in order:
             core_out[k] = gradient(k, 1).astype(bf16)
             csum_copy(k).start()
-        for k in reversed(range(1, planes)):
+
+    def send_out():
+        for k in order[:-1]:
             csum_copy(k).wait_recv()
             plane_out[k - 1] = (gradient(k, 0) + core_in[k].astype(f32)).astype(bf16)
             psum_copy(k).start()
+
+    @pl.when(holds)
+    def _():
+        for i in final:
+            for k in order:
+                pair(k, 1, src.at[i], i, True, k == order[0])
+        hand_over()
+        for i in final:
+            for k in order:
+                pair(k, 0, src.at[i], i, True, False)
+        send_out()
+        for i in final:
+            give_back(i)
+
+    @pl.when(joined & jnp.logical_not(holds))
+    def _():
+        hand_over()
+        send_out()
+
+    out_ref[...] = turned_gradient(own, mine)
+
+    @pl.when(joined)
+    def _():
         csum_copy(0).wait_recv()
-        mine_out[...] += gradient(0, 0) + core_in[0].astype(f32)
-        for k in range(1, planes):
+        out_ref[...] += gradient(0, 0) + core_in[0].astype(f32)
+        for k in order[:-1]:
             psum_copy(k).wait_recv()
-            mine_out[...] += plane_in[k - 1].astype(f32)
-
-    def gives(j):
-        return (rises & above(teams, team, j)) | (sinks & below(teams, team, j))
+            out_ref[...] += plane_in[k - 1].astype(f32)
 
     for j in range(teams):
-        @pl.when(gives(j))
+        @pl.when(uses(teams, team, j))
         def _():
             remote(line_out.at[j], line_in.at[j], lsum_send.at[j], lsum_recv.at[j], partner).wait_recv()
-            mine_out[...] += line_in[j].astype(f32)
-    put = pltpu.make_async_copy(mine_out, out_ref, out_sem)
-    put.start()
-    put.wait()
+            out_ref[...] += line_in[j].astype(f32)
 
     for k in range(1, planes):
         for h in range(2):
             plane_copy(k, h).wait_send()
     for k in range(planes):
         core_copy(k).wait_send()
-    for step, condition in ((1, rises), (-1, sinks)):
+    for step, condition in ways:
         @pl.when(condition)
         def _():
             for q in range(parts):
@@ -356,7 +458,7 @@
             for q in range(parts):
                 line_copy(i, q).wait_send()
 
-        @pl.when(uses(i, team))
+        @pl.when(used(i))
         def _():
             to_owner(i).wait_send()
 
@@ -378,7 +480,7 @@
         functools.partial(kernel, planes, teams, parts),
         out_shape=jax.ShapeDtypeStruct((rows, feat), jnp.float32),
         in_specs=[pl.BlockSpec(memory_space=pl.ANY)] * 3,
-        out_specs=pl.BlockSpec(memory_space=pl.ANY),
+        out_specs=pl.BlockSpec(memory_space=pltpu.VMEM),
         scratch_shapes=[
             pltpu.VMEM((3, rows, feat), kind),
             pltpu.VMEM((planes, 2, 3, rows, feat), kind),
@@ -394,8 +496,6 @@
             pltpu.VMEM((others, rows, feat), kind),
             pltpu.VMEM((teams, rows, feat), kind),
             pltpu.VMEM((teams, rows, feat), kind),
-            pltpu.VMEM((rows, feat), jnp.float32),
-            dma,
             dma((3,)),
             dma((planes,)), dma((planes,)),
             dma((planes, 2)), dma((planes, 2)),
@@ -405,8 +505,10 @@
             dma((planes,)), dma((planes,)),
             dma((teams,)), dma((teams,)),
         ],
-        compiler_params=pltpu.CompilerParams(collective_id=0, has_side_effects=True),
-    )(features, left_vectors, right_vectors)
+        compiler_params=pltpu.CompilerParams(
+            collective_id=0, has_side_effects=True, vmem_limit_bytes=24 * 2**20,
+        ),
+    )(*(pltpu.with_memory_space_constraint(v, pltpu.HBM) for v in (features, left_vectors, right_vectors)))
 
 
 def solution(mesh):

time: 32.8 us -> 26.5 us (0.81)
  the two profiles are of different devices: /device:TPU:17 before, /device:TPU:8 now
where the time goes in v2:
time: 26.5 us; the launch traced here: 26.4 us
  Pallas kernels  25.7 us (97%)
  local copies, waits for them, and re-layouts  0.66 us (2%)
    pallas_call x1, Pallas kernels, local(): pl.pallas_call(functools.partial(kernel, planes, teams, parts), out_shape...  25.7 us
    unnamed x1, local copies, waits for them, and re-layouts  0.66 us

profile of v2, /device:TPU:8, one launch (start us, length us, event | category | flops | bytes accessed | tf_op | source)
XLA Modules:
  0.0 26.4 jit_solution(9255546849659112628)
XLA Ops:
  0.0 25.7 %shard_map.37 = f32[256,128]{1,0:T(8,128)S(1)} custom-call(bf16[256,128]{1,0:T(8,128)(2,1)} %x_hbm.1, bf16[256,128]{1,0:T(8,128)(2,1)} %l_hbm.1, bf16[256,128]{1,0:T(8,128)(2,1)} %r_hbm.1), custom_call_target="tpu_custom_call" | custom-call | tf_op jit(solution)/shard_map/pallas_call | solution.py:479
  25.7 0.7 %copy.5 = f32[256,128]{1,0:T(8,128)} copy(f32[256,128]{1,0:T(8,128)S(1)} %shard_map.37) | data formatting | bytes 262144

commit v3 on v2

--- a/solution.py
+++ b/solution.py
@@ -158,12 +158,17 @@
 
     ways = ((1, rises(teams, team)), (-1, sinks(teams, team)))
 
-    def pass_on(q, condition):
-        for i in sources:
-            @pl.when(passes(i) & condition)
-            def _():
-                line_copy(i, q).wait_recv()
-                line_copy(i, q).start()
+    def pass_on(steps, condition):
+        @pl.when(condition)
+        def _():
+            for step in steps:
+                for i in sources:
+                    q = step - (direction(i) < 0)
+                    if 0 <= q < parts:
+                        @pl.when(passes(i))
+                        def _():
+                            line_copy(i, q).wait_recv()
+                            line_copy(i, q).start()
 
     on_line = jnp.minimum(team, 1) + jnp.minimum(teams - 1 - team, 1)
     pl.semaphore_wait(barrier, len(near) + on_line)
@@ -207,29 +212,51 @@
 
     mine = teams
 
-    def pair(k, c, ref, slot, add, first):
-        right = src_right[slot]
+    def products(k, c, ref, slot):
         target = raw(k, c)
-        dist = lax.dot_general(tgt_left[k, c], right, NT, preferred_element_type=f32)
+        dist = lax.dot_general(
+            tgt_left[k, c], src_right[slot], NT, preferred_element_type=f32,
+        )
         couple = lax.dot_general(
             jnp.concatenate([target[1], target[2]], axis=1),
             jnp.concatenate([ref[2], ref[1]], axis=1),
             NT, preferred_element_type=f32,
         )
+        return dist, couple
+
+    def weight_of(dist, couple):
         dist = jnp.maximum(dist, 1e-30)
         power = dist * lax.rsqrt(dist) * (-RATE)
-        weight = ((LOG2E - power) * jnp.exp2(power) * couple).astype(bf16)
+        return ((LOG2E - power) * jnp.exp2(power) * couple).astype(bf16)
+
+    def gather(k, c, slot, weight, add, first):
         back = jnp.dot(tgt_turned[k, c], weight, preferred_element_type=f32)
         if first:
             turned[slot] = back
         else:
             turned[slot] += back
         if add is not None:
-            forth = jnp.dot(weight, right, preferred_element_type=f32)
+            forth = jnp.dot(weight, src_right[slot], preferred_element_type=f32)
             if add:
                 acc[k, c] += forth
             else:
                 acc[k, c] = forth
+
+    def chain(jobs):
+        ahead = None
+        for n, (k, c, ref, slot, add, first) in enumerate(jobs):
+            now = products(k, c, ref, slot) if ahead is None else ahead
+            if n + 1 < len(jobs):
+                ahead = products(*jobs[n + 1][:4])
+            gather(k, c, slot, weight_of(*now), add, first)
+
+    def with_own(targets):
+        return [(k, c, own, mine, None, (k, c) == (0, 0)) for k, c in targets]
+
+    def with_source(i, targets, add, opens=False):
+        return [
+            (k, c, src.at[i], i, add, opens and n == 0) for n, (k, c) in enumerate(targets)
+        ]
 
     def gradient(k, c):
         total = acc[k, c]
@@ -270,16 +297,13 @@
                     line_copy(i, q).wait_recv()
             prepare_source(src.at[i], i)
 
-    def own_pairs(targets):
+    def prepare(targets):
         for k, c in targets:
             prepare_target(k, c)
-            pair(k, c, own, mine, None, (k, c) == (0, 0))
-
-    def pairs(i, targets):
-        @pl.when(used(i))
-        def _():
-            for k, c in targets:
-                pair(k, c, src.at[i], i, i > 0, (k, c) == targets[0] and (k, c) in opening)
+
+    def own_pairs(targets):
+        prepare(targets)
+        chain(with_own(targets))
 
     def to_owner(i):
         return remote(
@@ -301,24 +325,34 @@
     close = [(0, 0), (0, 1)] + [(k, 0) for k in single]
     across = [(k, 1) for k in single]
     rest = [(k, c) for c in (0, 1) for k in joint]
-    opening = close[:1]
     two = [k for k in joint if bin(k).count("1") == 2]
     more = [k for k in joint if k not in two]
 
     prepare_source(own, mine)
     own_pairs(close[:1])
-    pass_on(0, always)
+    pass_on(range(parts // 4), always)
     core_copy(0).wait_recv()
     own_pairs(close[1:2])
+    pass_on(range(parts // 4, parts // 2), low_half)
     for k in two:
         hand_on(k)
-    for q in range(1, parts - 1):
-        pass_on(q, always)
-    pass_on(parts - 1, low_half)
+    pass_on(range(parts // 2, parts + 1), low_half)
+    base = sources[:1]
+    ready = (team > 0) & low_half & (team < teams - 1)
+
+    @pl.when(ready)
+    def _():
+        for i in base:
+            take(i)
+            chain(with_source(i, close[:2], False, True))
+    pass_on(range(parts // 4, 3 * parts // 4), jnp.logical_not(low_half))
     for k in single:
         relay(k)
-    pass_on(parts - 1, jnp.logical_not(low_half))
-    own_pairs(close[2:])
+
+    @pl.when(jnp.logical_not(ready))
+    def _():
+        own_pairs(close[2:])
+    pass_on(range(3 * parts // 4, parts + 1), jnp.logical_not(low_half))
 
     end = team == teams - 1
 
@@ -331,69 +365,86 @@
                 core_copy(k).start()
 
     relay_rest(end)
-    base = sources[:1]
     inner = sources[1:-1]
     final = sources[1:][-1:]
     alone, joined = team == 0, team > 0
 
-    def own_and_base(targets):
-        @pl.when(alone)
-        def _():
-            own_pairs(targets)
-
-        @pl.when(joined)
-        def _():
-            own_pairs(targets)
-            for i in base:
-                for k, c in targets:
-                    pair(k, c, src.at[i], i, False, False)
-
+    between = joined & jnp.logical_not(end)
+
+    @pl.when(ready)
+    def _():
+        prepare(close[2:])
+        jobs = with_own(close[2:])
+        for i in base:
+            jobs += with_source(i, close[2:], False)
+        chain(jobs)
     for i in base:
+        @pl.when(between & jnp.logical_not(ready))
+        def _():
+            take(i)
+            chain(with_source(i, close, False, True))
+    for i in inner:
         take(i)
-        pairs(i, close)
+
+        @pl.when(used(i))
+        def _():
+            chain(with_source(i, close, True, True))
+    beside = (used(final[0]) & (abs(final[0] - team) == 1)) if final else team < 0
+    for i in final:
+        @pl.when(beside)
+        def _():
+            take(i)
+            chain(with_source(i, close, True, True))
     relay_rest(jnp.logical_not(end))
     for k in two:
         arrived.update({(k, 0), (k, 1)})
     for k in more:
         hand_on(k)
         relay(k)
-    for i in inner:
-        take(i)
-        pairs(i, close)
     for k, c in across:
         core_copy(k).wait_recv()
-    if across:
-        own_and_base(across)
+
+    @pl.when(jnp.logical_not(between))
+    def _():
+        own_pairs(across)
+
+    @pl.when(between)
+    def _():
+        prepare(across)
+        chain(with_own(across) + [job for i in base for job in with_source(i, across, False)])
+
     for k, c in rest:
         if c:
             core_copy(k).wait_recv()
 
-    @pl.when(alone)
+    @pl.when(jnp.logical_not(between))
     def _():
         own_pairs(rest)
 
-    @pl.when(joined)
-    def _():
-        for k, c in rest:
-            prepare_target(k, c)
-            for i in base:
-                pair(k, c, src.at[i], i, False, False)
+    @pl.when(joined & end)
+    def _():
         for i in base:
+            take(i)
+            chain(with_source(i, close + across + rest, False, True))
             give_back(i)
 
-    @pl.when(joined)
-    def _():
-        for k, c in rest:
-            pair(k, c, own, mine, None, False)
+    @pl.when(between)
+    def _():
+        prepare(rest)
+        for i in base:
+            chain(with_source(i, rest, False))
+            give_back(i)
+        chain(with_own(rest))
     for i in inner:
-        pairs(i, across + rest)
-
         @pl.when(used(i))
         def _():
+            chain(with_source(i, across + rest, True))
             give_back(i)
 
     for i in final:
-        take(i)
+        @pl.when(jnp.logical_not(beside))
+        def _():
+            take(i)
     order = list(reversed(range(planes)))
     holds = used(final[0]) if final else team < 0
 
@@ -408,18 +459,22 @@
             plane_out[k - 1] = (gradient(k, 0) + core_in[k].astype(f32)).astype(bf16)
             psum_copy(k).start()
 
-    @pl.when(holds)
-    def _():
-        for i in final:
-            for k in order:
-                pair(k, 1, src.at[i], i, True, k == order[0])
-        hand_over()
-        for i in final:
-            for k in order:
-                pair(k, 0, src.at[i], i, True, False)
-        send_out()
-        for i in final:
-            give_back(i)
+    def finish(condition, done):
+        @pl.when(condition)
+        def _():
+            for i in final:
+                targets = [(k, 1) for k in order if (k, 1) not in done]
+                chain(with_source(i, targets, True, not done))
+            hand_over()
+            for i in final:
+                targets = [(k, 0) for k in order if (k, 0) not in done]
+                chain(with_source(i, targets, True))
+            send_out()
+            for i in final:
+                give_back(i)
+
+    finish(holds & beside, close)
+    finish(holds & jnp.logical_not(beside), [])
 
     @pl.when(joined & jnp.logical_not(holds))
     def _():
@@ -474,7 +529,7 @@
     rows, feat = features.shape
     kind = jnp.bfloat16
     dma = pltpu.SemaphoreType.DMA
-    parts = 4
+    parts = math.gcd(rows // 16, 4)
     others = max(planes - 1, 1)
     return pl.pallas_call(
         functools.partial(kernel, planes, teams, parts),

time: 26.5 us -> 24.5 us (0.925); the launches traced: 26.4 us -> 24.1 us
  Pallas kernels: 25.7 us -> 23.4 us
    pallas_call x1, Pallas kernels: 25.7 us -> 23.4 us  [local(): pl.pallas_call(functools.partial(kernel, planes, teams, parts), out_shape...]
where the time goes in v3:
time: 24.5 us; the launch traced here: 24.1 us
  Pallas kernels  23.4 us (96%)
  local copies, waits for them, and re-layouts  0.66 us (3%)
    pallas_call x1, Pallas kernels, local(): pl.pallas_call(functools.partial(kernel, planes, teams, parts), out_shape...  23.4 us
    unnamed x1, local copies, waits for them, and re-layouts  0.66 us

profile of v3, /device:TPU:8, one launch (start us, length us, event | category | flops | bytes accessed | tf_op | source)
XLA Modules:
  0.0 24.1 jit_solution(2081300831635806335)
XLA Ops:
  0.0 23.4 %shard_map.37 = f32[256,128]{1,0:T(8,128)S(1)} custom-call(bf16[256,128]{1,0:T(8,128)(2,1)} %x_hbm.1, bf16[256,128]{1,0:T(8,128)(2,1)} %l_hbm.1, bf16[256,128]{1,0:T(8,128)(2,1)} %r_hbm.1), custom_call_target="tpu_custom_call" | custom-call | tf_op jit(solution)/shard_map/pallas_call | solution.py:534
  23.4 0.7 %copy.5 = f32[256,128]{1,0:T(8,128)} copy(f32[256,128]{1,0:T(8,128)S(1)} %shard_map.37) | data formatting | bytes 262144

commit v4 on v3

--- a/solution.py
+++ b/solution.py
@@ -242,13 +242,15 @@
             else:
                 acc[k, c] = forth
 
-    def chain(jobs):
+    def chain(jobs, after=None, then=None):
         ahead = None
         for n, (k, c, ref, slot, add, first) in enumerate(jobs):
             now = products(k, c, ref, slot) if ahead is None else ahead
             if n + 1 < len(jobs):
                 ahead = products(*jobs[n + 1][:4])
             gather(k, c, slot, weight_of(*now), add, first)
+            if n + 1 == after:
+                then()
 
     def with_own(targets):
         return [(k, c, own, mine, None, (k, c) == (0, 0)) for k, c in targets]
@@ -374,10 +376,8 @@
     @pl.when(ready)
     def _():
         prepare(close[2:])
-        jobs = with_own(close[2:])
         for i in base:
-            jobs += with_source(i, close[2:], False)
-        chain(jobs)
+            chain(with_source(i, close[2:], False))
     for i in base:
         @pl.when(between & jnp.logical_not(ready))
         def _():
@@ -401,41 +401,69 @@
     for k in more:
         hand_on(k)
         relay(k)
+    never = team < 0
+    lone, others = (inner, []) if len(inner) == 1 else ([], inner)
+    rich = (between & used(lone[0])) if lone else never
+    side = between & beside & jnp.logical_not(rich)
+    plain = between & jnp.logical_not(rich) & jnp.logical_not(side)
+    modes = ((rich, lone), (side, final), (plain, []))
     for k, c in across:
         core_copy(k).wait_recv()
 
-    @pl.when(jnp.logical_not(between))
+    @pl.when(alone)
     def _():
         own_pairs(across)
 
-    @pl.when(between)
-    def _():
-        prepare(across)
-        chain(with_own(across) + [job for i in base for job in with_source(i, across, False)])
+    for mode, more_sources in modes:
+        @pl.when(mode)
+        def _():
+            prepare(across)
+            jobs = []
+            for i in base:
+                jobs += with_source(i, across, False)
+            for i in more_sources:
+                jobs += with_source(i, across, True)
+            chain(jobs)
 
     for k, c in rest:
         if c:
             core_copy(k).wait_recv()
 
-    @pl.when(jnp.logical_not(between))
+    @pl.when(alone)
     def _():
         own_pairs(rest)
 
+    def base_back():
+        for i in base:
+            give_back(i)
+
     @pl.when(joined & end)
     def _():
+        prepare(across + rest)
         for i in base:
             take(i)
             chain(with_source(i, close + across + rest, False, True))
-            give_back(i)
-
-    @pl.when(between)
+        base_back()
+
+    @pl.when(plain | side)
     def _():
         prepare(rest)
         for i in base:
             chain(with_source(i, rest, False))
+        base_back()
+
+    @pl.when(rich)
+    def _():
+        prepare(rest)
+        jobs = []
+        for i in base:
+            jobs += with_source(i, rest, False)
+        for i in lone:
+            jobs += with_source(i, rest, True)
+        chain(jobs, len(rest), base_back)
+        for i in lone:
             give_back(i)
-        chain(with_own(rest))
-    for i in inner:
+    for i in others:
         @pl.when(used(i))
         def _():
             chain(with_source(i, across + rest, True))
@@ -459,27 +487,44 @@
             plane_out[k - 1] = (gradient(k, 0) + core_in[k].astype(f32)).astype(bf16)
             psum_copy(k).start()
 
-    def finish(condition, done):
+    def finish(condition, done, own_between):
         @pl.when(condition)
         def _():
             for i in final:
                 targets = [(k, 1) for k in order if (k, 1) not in done]
                 chain(with_source(i, targets, True, not done))
             hand_over()
+            jobs = []
             for i in final:
                 targets = [(k, 0) for k in order if (k, 0) not in done]
-                chain(with_source(i, targets, True))
+                jobs += with_source(i, targets, True)
+            chain(jobs + with_own(own_between))
             send_out()
             for i in final:
                 give_back(i)
 
-    finish(holds & beside, close)
-    finish(holds & jnp.logical_not(beside), [])
+    finish(side, close + across, across)
+    finish(holds & beside & jnp.logical_not(side), close, [])
+    finish(holds & jnp.logical_not(beside), [], [])
 
     @pl.when(joined & jnp.logical_not(holds))
     def _():
         hand_over()
+
+        @pl.when(end)
+        def _():
+            chain(with_own(across + rest))
         send_out()
+
+    for mode, targets in (
+        (ready & jnp.logical_not(side), close[2:] + across + rest),
+        (ready & side, close[2:] + rest),
+        (between & jnp.logical_not(ready) & side, rest),
+        (between & jnp.logical_not(ready) & jnp.logical_not(side), across + rest),
+    ):
+        @pl.when(mode)
+        def _():
+            chain(with_own(targets))
 
     out_ref[...] = turned_gradient(own, mine)
 

time: 24.5 us -> 23.8 us (0.971)
  Pallas kernels: 23.4 us -> 22.7 us
    pallas_call x1, Pallas kernels: 23.4 us -> 22.7 us  [local(): pl.pallas_call(functools.partial(kernel, planes, teams, parts), out_shape...]
where the time goes in v4:
time: 23.8 us; the launch traced here: 23.4 us
  Pallas kernels  22.7 us (95%)
  local copies, waits for them, and re-layouts  0.66 us (3%)
    pallas_call x1, Pallas kernels, local(): pl.pallas_call(functools.partial(kernel, planes, teams, parts), out_shape...  22.7 us
    unnamed x1, local copies, waits for them, and re-layouts  0.66 us

profile of v4, /device:TPU:8, one launch (start us, length us, event | category | flops | bytes accessed | tf_op | source)
XLA Modules:
  0.0 23.4 jit_solution(1114678731010663394)
XLA Ops:
  0.0 22.7 %shard_map.37 = f32[256,128]{1,0:T(8,128)S(1)} custom-call(bf16[256,128]{1,0:T(8,128)(2,1)} %x_hbm.1, bf16[256,128]{1,0:T(8,128)(2,1)} %l_hbm.1, bf16[256,128]{1,0:T(8,128)(2,1)} %r_hbm.1), custom_call_target="tpu_custom_call" | custom-call | tf_op jit(solution)/shard_map/pallas_call | solution.py:579
  22.7 0.7 %copy.5 = f32[256,128]{1,0:T(8,128)} copy(f32[256,128]{1,0:T(8,128)S(1)} %shard_map.37) | data formatting | bytes 262144
